TPU v7x, 32 devices: a whole 2x2x4 slice. The times are simulated.
32 devices in a mesh: wide: 8 (over z, x), narrow: 4 (over y, core).
Axes of the slice: x: 2, y: 2, z: 4, core: 2. Of those that a mesh axis runs over, the one named last changes fastest.
Arguments:
- hidden: bfloat16 [512, 4096], P('narrow', 'wide'), may hold values from -6 to 6
- attn_gain: float32 [4096], replicated, may hold values from 0.5 to 1.5
- query_weight: bfloat16 [4096, 4096], P(None, 'wide'), may hold values from -0.09375 to 0.09375
- key_weight: bfloat16 [4096, 1024], P('wide'), may hold values from -0.125 to 0.125
- value_weight: bfloat16 [4096, 1024], P('wide'), may hold values from -0.125 to 0.125
- out_weight: bfloat16 [4096, 4096], P('wide'), may hold values from -0.09375 to 0.09375
- cache_key: bfloat16 [8, 512, 128], replicated, may hold values from -600 to 600
- cache_value: bfloat16 [8, 512, 128], replicated, may hold values from -6 to 6
- mlp_gain: float32 [4096], replicated, may hold values from 0.5 to 1.5
- router_weight: bfloat16 [4096, 16], replicated, may hold values from -0.09375 to 0.09375
- expert_ids: int32 [512, 2], P('narrow'), may hold values from 0 to 15, all different within a row; in each aligned block of 16 rows (0 to 15, 16 to 31, ...) at most 4 rows name the same one
- gate_weight: bfloat16 [32, 4096, 3200], P('wide', None, 'narrow'), may hold values from -0.09375 to 0.09375
- up_weight: bfloat16 [32, 4096, 3200], P('wide', None, 'narrow'), may hold values from -0.09375 to 0.09375
- down_weight: bfloat16 [32, 3200, 4096], P('wide', 'narrow'), may hold values from -0.078125 to 0.078125
Outputs:
- layer_out: bfloat16 [512, 4096], P('narrow', 'wide')
Inputs may be any that keep to these rules, and one draw needn't show every extreme that they name: `expert_ids`: in each aligned block of 16 rows no expert is named by more than 4 rows, and in every block some expert by exactly 4; the two experts of a row differ.
All inputs are finite; a program needn't handle non-finite values.
Results may differ from a plain program's by a relative error of at most 0.012.
The roundings to bfloat16 on the way count: a program that leaves them out, or rounds other values in their place, can miss the bound.
Values may be sent and summed in bfloat16 or wider, within the bound.
No kernel may reach another device: no remote copies, remote signals or barrier semaphores. Data moves between devices by JAX's collectives and lax.ppermute only.
A program may use at most 192 MiB of HBM per device.

v0:
```python
import jax
import jax.numpy as jnp
from jax import lax
from jax.sharding import PartitionSpec as P

SPLIT = 2
CAPD = 4
epsilon = 1e-05


def layer_normed(values, gain):
    average = jnp.mean(values, axis=-1, keepdims=True)
    centered = values - average
    variance = jnp.mean(centered * centered, axis=-1, keepdims=True)
    return centered * lax.rsqrt(variance + epsilon) * gain


def slot_targets(routing, experts, capacity):
    blocks = routing.shape[0]
    flat_ids = routing.reshape(blocks, -1)
    onehot = (flat_ids[:, :, None] == jnp.arange(experts, dtype=jnp.int32)[None, None, :]).astype(
        jnp.int32
    )
    earlier = jnp.cumsum(onehot, axis=1) - onehot
    position = jnp.sum(earlier * onehot, axis=2)
    return (flat_ids * capacity + position).reshape(routing.shape)


def fill_buffer(normed, target, slot_count):
    matches = (target[:, :, :, None] == jnp.arange(slot_count, dtype=jnp.int32)).astype(
        jnp.bfloat16
    )
    placing = jnp.sum(matches, axis=2)
    return jnp.einsum("btj,btd->bjd", placing, normed, preferred_element_type=jnp.float32).astype(
        jnp.bfloat16
    )


def pair_weights(logits, routing):
    picked = jnp.take_along_axis(logits, routing, axis=-1)
    leading = jax.nn.sigmoid(picked[..., 0] - picked[..., 1])
    return jnp.stack([leading, 1.0 - leading], axis=-1)


def gather_back(results, target, weights):
    blocks, slot_count = (results.shape[0], results.shape[1])
    flat_rows = results.reshape(blocks * slot_count, results.shape[2])
    row_index = target + (jnp.arange(blocks, dtype=jnp.int32) * slot_count)[:, None, None]
    picked = jnp.take(flat_rows, row_index.reshape(-1), axis=0).reshape(
        target.shape + (results.shape[2],)
    )
    return jnp.sum(picked * weights[..., None], axis=2)


def expert_terms(arrived, w_gate, w_up, w_down):
    gate_term = jnp.einsum("gscd,sdf->gscf", arrived, w_gate, preferred_element_type=jnp.float32)
    up_term = jnp.einsum("gscd,sdf->gscf", arrived, w_up, preferred_element_type=jnp.float32)
    active = (jax.nn.silu(gate_term) * up_term).astype(jnp.bfloat16)
    return jnp.einsum("gscf,sfd->gscd", active, w_down, preferred_element_type=jnp.float32)


def attend(queries, all_keys, all_values, first_row, context):
    row_count, heads_here, head_size = queries.shape
    kv_here = all_keys.shape[0]
    grouped = queries.reshape(row_count, kv_here, heads_here // kv_here, head_size)
    scale_factor = head_size ** (-0.5)
    scores = (
        jnp.einsum("rgqd,gkd->gqrk", grouped, all_keys, preferred_element_type=jnp.float32)
        * scale_factor
    )
    row_ids = first_row + jnp.arange(row_count, dtype=jnp.int32)
    key_ids = jnp.arange(all_keys.shape[1], dtype=jnp.int32) - context
    allowed = key_ids[None, :] <= row_ids[:, None]
    scores = jnp.where(allowed[None, None], scores, -1e30)
    highest = jnp.max(scores, axis=3, keepdims=True)
    weights = jnp.exp(scores - highest)
    weights = (weights / jnp.sum(weights, axis=3, keepdims=True)).astype(jnp.bfloat16)
    mixed = jnp.einsum(
        "gqrk,gkd->rgqd", weights, all_values, preferred_element_type=jnp.float32
    ).astype(jnp.bfloat16)
    return mixed.reshape(row_count, heads_here, head_size)


def body(
    hidden,
    attn_gain,
    query_weight,
    key_weight,
    value_weight,
    out_weight,
    cache_key,
    cache_value,
    mlp_gain,
    router_weight,
    expert_ids,
    gate_weight,
    up_weight,
    down_weight,
):
    wide_count = lax.axis_size("wide")
    wide_index = lax.axis_index("wide")
    narrow_index = lax.axis_index("narrow")
    full_rows = lax.all_gather(hidden, "wide", axis=1, tiled=True)
    row_count, feature_count = full_rows.shape
    kv_total, context, head_size = cache_key.shape
    heads_here = query_weight.shape[1] // head_size
    share = heads_here * wide_count // kv_total
    kv_here = max(heads_here // share, 1)
    kv_start = wide_index * heads_here // share
    normed = layer_normed(full_rows.astype(jnp.float32), attn_gain).astype(jnp.bfloat16)
    queries = jnp.dot(normed, query_weight, preferred_element_type=jnp.float32).astype(jnp.bfloat16)
    feature_share = key_weight.shape[0]
    normed_part = lax.dynamic_slice_in_dim(normed, wide_index * feature_share, feature_share, 1)
    key_term = jnp.dot(normed_part, key_weight, preferred_element_type=jnp.float32)
    value_term = jnp.dot(normed_part, value_weight, preferred_element_type=jnp.float32)
    key_cols, value_cols = lax.psum((key_term, value_term), "wide")
    key_cols = key_cols.astype(jnp.bfloat16)
    value_cols = value_cols.astype(jnp.bfloat16)
    fresh_keys = lax.dynamic_slice_in_dim(key_cols, kv_start * head_size, kv_here * head_size, 1)
    fresh_values = lax.dynamic_slice_in_dim(
        value_cols, kv_start * head_size, kv_here * head_size, 1
    )
    span_key_rows, span_value_rows = (
        lax.all_gather(fresh_keys, "narrow", axis=0, tiled=True),
        lax.all_gather(fresh_values, "narrow", axis=0, tiled=True),
    )
    own_cache_key = lax.dynamic_slice_in_dim(cache_key, kv_start, kv_here, 0)
    own_cache_value = lax.dynamic_slice_in_dim(cache_value, kv_start, kv_here, 0)
    all_keys = jnp.concatenate(
        [own_cache_key, span_key_rows.reshape(-1, kv_here, head_size).transpose(1, 0, 2)], axis=1
    )
    all_values = jnp.concatenate(
        [own_cache_value, span_value_rows.reshape(-1, kv_here, head_size).transpose(1, 0, 2)],
        axis=1,
    )
    attended = attend(
        queries.reshape(row_count, heads_here, head_size),
        all_keys,
        all_values,
        narrow_index * row_count,
        context,
    )
    attended = attended.reshape(row_count, heads_here * head_size)
    experts = router_weight.shape[1]
    capacity = CAPD
    slot_count = experts * SPLIT
    slots_here = gate_weight.shape[0]
    block_rows = row_count // wide_count
    head_mix = lax.psum_scatter(
        jnp.dot(attended, out_weight, preferred_element_type=jnp.float32),
        "wide",
        scatter_dimension=0,
        tiled=True,
    )
    own_rows = lax.dynamic_slice_in_dim(full_rows, wide_index * block_rows, block_rows, 0)
    residual = (own_rows.astype(jnp.float32) + head_mix).astype(jnp.bfloat16)
    normed_two = layer_normed(residual.astype(jnp.float32), mlp_gain).astype(jnp.bfloat16)
    logits = jnp.dot(normed_two, router_weight, preferred_element_type=jnp.float32)[None]
    routing = lax.dynamic_slice_in_dim(expert_ids, wide_index * block_rows, block_rows, 0)[None]
    target = slot_targets(routing, experts, capacity)
    buffer = fill_buffer(normed_two[None], target, experts * capacity)
    buffer = jnp.broadcast_to(
        buffer.reshape(experts, 1, capacity, feature_count),
        (experts, SPLIT, capacity, feature_count),
    )
    arrived = lax.all_to_all(
        buffer.reshape(slot_count, capacity, feature_count),
        "wide",
        split_axis=0,
        concat_axis=0,
        tiled=True,
    )
    arrived = arrived.reshape(wide_count, slots_here, capacity, feature_count)
    partial_out = expert_terms(
        lax.all_gather(arrived, "narrow", axis=0, tiled=True), gate_weight, up_weight, down_weight
    )
    reduced = lax.psum_scatter(partial_out, "narrow", scatter_dimension=0, tiled=True).astype(
        jnp.bfloat16
    )
    returned = lax.all_to_all(reduced, "wide", split_axis=0, concat_axis=1, tiled=True)
    summed = jnp.sum(
        returned.reshape(1, experts, SPLIT, capacity, feature_count).astype(jnp.float32), axis=2
    )
    mixture = gather_back(
        summed.reshape(1, experts * capacity, feature_count), target, pair_weights(logits, routing)
    )
    result = (residual.astype(jnp.float32) + mixture[0]).astype(jnp.bfloat16)
    final_out = lax.all_to_all(result, "wide", split_axis=1, concat_axis=0, tiled=True)
    return final_out


def solution(mesh):
    placed = (
        P("narrow", "wide"),
        P(),
        P(None, "wide"),
        P("wide", None),
        P("wide", None),
        P("wide", None),
        P(),
        P(),
        P(),
        P(),
        P("narrow", None),
        P("wide", None, "narrow"),
        P("wide", None, "narrow"),
        P("wide", "narrow", None),
    )
    return jax.shard_map(
        body, mesh=mesh, in_specs=placed, out_specs=P("narrow", "wide"), check_vma=False
    )
```

profile of v0, /device:TPU:0, one launch (start us, length us, event | category | flops | bytes accessed | tf_op | source)
XLA Modules:
  0.0 455.7 jit_solution(893464131646840608)
XLA Ops:
  6.5 0.7 all-gather.3.cloned.1.call-update
  7.4 0.9 constant_dynamic-slice_fusion.1
  8.3 0.9 constant_dynamic-slice_fusion.2
  9.4 42.1 %all-gather.3.cloned.1.call-done = bf16[128,4096]{1,0:T(8,128)(2,1)} async-done(((bf16[128,512]{1,0:T(8,128)(2,1)}), bf16[128,4096]{1,0:T(8,128)(2,1)}) %all-gather.3.cloned.1.call-update) | async-done | bytes 1048592 | tf_op jit(solution)/shard_map/all_gather | solution.py:103
  51.5 1.5 convert_reduce_fusion
  53.1 1.7 fusion.11
  55.2 3.0 fusion.21
  58.5 0.9 copy-done.4
  59.7 71.9 %all-reduce.2 = (bf16[128,1024]{1,0:T(8,128)(2,1)S(1)}, bf16[128,1024]{1,0:T(8,128)(2,1)S(1)}) all-reduce(f32[128,1024]{1,0:T(8,128)S(1)} %fusion.35, f32[128,1024]{1,0:T(8,128)S(1)} %fusion.37), channel_id=1, replica_groups=mesh['wide'=8,'narrow'=4] {'wide'}, use_global_device_ids=true, to_apply=%region_3.4 | all-reduce | flops 262144 | bytes 1572864 | tf_op jit(solution)/shard_map/psum | solution.py:116
  131.6 5.4 %all_gather.14 = bf16[512,128]{1,0:T(8,128)(2,1)S(1)} all-gather(bf16[128,128]{1,0:T(8,128)(2,1)S(1)} %dynamic-slice_convert_fusion), channel_id=1, replica_groups=mesh['wide'=8,'narrow'=4] {'narrow'}, dimensions={0}, use_global_device_ids=true | all-gather | bytes 163840 | tf_op jit(solution)/shard_map/all_gather | solution.py:124
  137.0 5.4 %all_gather.13 = bf16[512,128]{1,0:T(8,128)(2,1)S(1)} all-gather(bf16[128,128]{1,0:T(8,128)(2,1)S(1)} %dynamic-slice_convert_fusion.1), channel_id=1, replica_groups=mesh['wide'=8,'narrow'=4] {'narrow'}, dimensions={0}, use_global_device_ids=true | all-gather | bytes 163840 | tf_op jit(solution)/shard_map/all_gather | solution.py:125
  143.8 1.6 copy-done.3
  145.4 2.1 fusion.54
  149.0 67.0 %reduce-scatter.3.cloned.1.call-done = f32[16,4096]{1,0:T(8,128)} async-done(((f32[128,4096]{1,0:T(8,128)}), f32[16,4096]{1,0:T(8,128)}) %reduce-scatter.3.cloned.1.call-update) | async-done | bytes 262160 | tf_op jit(solution)/shard_map/reduce_scatter | solution.py:149
  216.0 1.1 convert_reduce_fusion.2
  218.3 27.7 %all_to_all.33 = bf16[32,4,4096]{2,1,0:T(4,128)(2,1)S(1)} all-to-all(bf16[32,4,4096]{2,1,0:T(4,128)(2,1)S(1)} %bitcast.107), channel_id=1, replica_groups=mesh['wide'=8,'narrow'=4] {'wide'}, dimensions={0} | all-to-all | bytes 2097152 | tf_op jit(solution)/shard_map/all_to_all | solution.py:166
  246.0 1.6 copy.64
  247.8 33.3 %all-gather.5.cloned.1.call-done = bf16[32,4,4,4096]{3,0,2,1:T(8,128)(2,1)} async-done(((bf16[8,4,4,4096]{3,0,2,1:T(8,128)(2,1)}), bf16[32,4,4,4096]{3,0,2,1:T(8,128)(2,1)}) %all-gather.5.cloned.1.call-update) | async-done | bytes 4194320 | tf_op jit(solution)/shard_map/all_gather | solution.py:175
  281.1 16.0 %fusion.4 = f32[4,32,4,800]{3,1,2,0:T(8,128)} fusion(bf16[32,4,4,4096]{3,0,2,1:T(8,128)(2,1)} %all-gather.5.cloned.1.call-done, bf16[4,4096,800]{1,2,0:T(8,128)(2,1)} %param.25), kind=kOutput, calls=%fused_computation.6 | convolution fusion | flops 3355443200 | bytes 32047104 | tf_op jit(solution)/shard_map/gscd,sdf->gscf/dot_general | solution.py:56
  297.2 15.3 %fusion.15 = bf16[32,4,4,800]{3,0,2,1:T(8,128)(2,1)S(1)} fusion(f32[4,32,4,800]{3,1,2,0:T(8,128)} %fusion.4, bf16[32,4,4,4096]{3,0,2,1:T(8,128)(2,1)} %all-gather.5.cloned.1.call-done, bf16[4,4096,800]{1,2,0:T(8,128)(2,1)} %param.26), kind=kOutput, calls=%fused_computation.23 | convolution fusion | flops 3357900800 | bytes 32866304 | tf_op jit(solution)/shard_map/gscd,sdf->gscf/dot_general | solution.py:57
  312.5 16.2 %fusion.6 = f32[32,4,4,4096]{3,0,2,1:T(8,128)} fusion(bf16[32,4,4,800]{3,0,2,1:T(8,128)(2,1)S(1)} %fusion.15, bf16[4,800,4096]{2,1,0:T(8,128)(2,1)} %param.27), kind=kOutput, calls=%fused_computation.8 | convolution fusion | flops 3355443200 | bytes 35422208 | tf_op jit(solution)/shard_map/gscf,sfd->gscd/dot_general | solution.py:59
  328.7 71.5 %reduce-scatter.5.cloned.1.call-done = f32[8,4,4,4096]{3,0,2,1:T(8,128)} async-done(((f32[32,4,4,4096]{3,0,2,1:T(8,128)}), f32[8,4,4,4096]{3,0,2,1:T(8,128)}) %reduce-scatter.5.cloned.1.call-update) | async-done | bytes 2097168 | tf_op jit(solution)/shard_map/reduce_scatter | solution.py:177
  400.2 1.7 convert_element_type.112
  402.0 1.8 copy.65
  403.8 5.5 %all-to-all-start.1 = ((bf16[8,4,4,4096]{3,2,1,0:T(4,128)(2,1)}), bf16[8,4,4,4096]{3,2,1,0:T(4,128)(2,1)S(1)}, u32[]{:S(2)}, u32[]{:S(2)}) async-start(bf16[8,4,4,4096]{3,2,1,0:T(4,128)(2,1)} %copy.65), calls=%async_computation.3 | async-start | bytes 2097152 | tf_op jit(solution)/shard_map/all_to_all | solution.py:180
  410.0 0.7 gather_fusion.1
  411.0 23.9 %all-to-all-done.1 = bf16[8,4,4,4096]{3,2,1,0:T(4,128)(2,1)S(1)} async-done(((bf16[8,4,4,4096]{3,2,1,0:T(4,128)(2,1)}), bf16[8,4,4,4096]{3,2,1,0:T(4,128)(2,1)S(1)}, u32[]{:S(2)}, u32[]{:S(2)}) %all-to-all-start.1) | async-done | bytes 1048608 | tf_op jit(solution)/shard_map/all_to_all | solution.py:180
  434.9 0.6 convert_reduce_fusion.1
  435.9 0.7 gather_fusion
  437.0 0.8 multiply_reduce_fusion
  437.8 10.7 %all_to_all.34 = bf16[16,8,512]{2,0,1:T(8,128)(2,1)S(1)} all-to-all(bf16[16,8,512]{2,0,1:T(8,128)(2,1)S(1)} %bitcast.109), channel_id=1, replica_groups=mesh['wide'=8,'narrow'=4] {'wide'}, dimensions={1} | all-to-all | bytes 262144 | tf_op jit(solution)/shard_map/all_to_all | solution.py:188
  448.5 0.7 copy.92
  (71 shorter events, 7.3 us)
Async XLA Ops:
  6.5 51.6 %copy-start = (bf16[512,1024]{1,0:T(8,128)(2,1)S(1)}, bf16[512,1024]{1,0:T(8,128)(2,1)}, u32[]{:S(2)}) copy-start(bf16[512,1024]{1,0:T(8,128)(2,1)} %param.17) | copy-start | bytes 3145732
  6.5 48.2 %copy-start.5 = (f32[4096]{0:T(1024)S(1)}, f32[4096]{0:T(1024)}, u32[]{:S(2)}) copy-start(f32[4096]{0:T(1024)} %param.15) | copy-start | bytes 49156
  6.5 45.0 %all-gather.3.cloned.1.call-start = ((), (), s32[]{:S(2)}) async-start(), calls=%async_computation.5 | async-start | bytes 1179648 | tf_op jit(solution)/shard_map/all_gather | solution.py:103
  7.3 208.7 %reduce-scatter.3.cloned.1.call-start = ((), (), s32[]{:S(2)}) async-start(), calls=%async_computation.6 | async-start | bytes 2359296 | tf_op jit(solution)/shard_map/reduce_scatter | solution.py:149
  51.5 3.2 copy-start.2
  58.1 1.2 copy-start.4
  143.2 2.2 copy-start.3
  147.5 0.7 copy-start.7
  147.5 69.8 %copy-start.6 = (f32[4096]{0:T(1024)S(1)}, f32[4096]{0:T(1024)}, u32[]{:S(2)}) copy-start(f32[4096]{0:T(1024)} %param.22) | copy-start | bytes 49156
  147.5 133.6 %all-gather.5.cloned.1.call-start = ((), (), s32[]{:S(2)}) async-start(), calls=%async_computation.7 | async-start | bytes 5242880 | tf_op jit(solution)/shard_map/all_gather | solution.py:175
  247.6 152.6 %reduce-scatter.5.cloned.1.call-start = ((), (), s32[]{:S(2)}) async-start(), calls=%async_computation.8 | async-start | bytes 10485760 | tf_op jit(solution)/shard_map/reduce_scatter | solution.py:177
  402.0 7.8 %copy-start.8 = (bf16[4096,16]{0,1:T(8,128)(2,1)S(1)}, bf16[4096,16]{0,1:T(8,128)(2,1)}, u32[]{:S(2)}) copy-start(bf16[4096,16]{0,1:T(8,128)(2,1)} %param.23) | copy-start | bytes 393220
  403.8 31.2 %all-to-all-start.1 = ((bf16[8,4,4,4096]{3,2,1,0:T(4,128)(2,1)}), bf16[8,4,4,4096]{3,2,1,0:T(4,128)(2,1)S(1)}, u32[]{:S(2)}, u32[]{:S(2)}) async-start(bf16[8,4,4,4096]{3,2,1,0:T(4,128)(2,1)} %copy.65), calls=%async_computation.3 | async-start | bytes 2097152 | tf_op jit(solution)/shard_map/all_to_all | solution.py:180
  435.9 13.3 %copy-start.1 = (bf16[512,1024]{1,0:T(8,128)(2,1)S(1)}, bf16[512,1024]{1,0:T(8,128)(2,1)}, u32[]{:S(2)}) copy-start(bf16[512,1024]{1,0:T(8,128)(2,1)} %param.17) | copy-start | bytes 3145732
Sparse Core Ops, SparseCore 0:
  9.4 42.1 all-gather.2
  147.6 68.2 reduce-scatter.2
  247.7 33.3 all-gather.4
  328.8 71.3 reduce-scatter.4
where the time goes:
time: 456 us
  waiting for transfers between devices  239 us (52%)
  blocking collectives  121 us (27%)
  matrix products  54.8 us (12%)
  between operations  13.5 us (3%)
  local copies, waits for them, and re-layouts  12.9 us (3%)
  other arithmetic  9.11 us (2%)
  starting transfers between devices  5.82 us (1%)
    psum x1, blocking collectives, body(): key_cols, value_cols = lax.psum((key_term, value_term), 'wide')  71.9 us
    reduce_scatter x1, waiting for transfers between devices, body(): lax.psum_scatter(partial_out, 'narrow', scatter_dimension=0, tiled=True)  71.5 us
    reduce_scatter x1, waiting for transfers between devices, body(): lax.psum_scatter(jnp.dot(attended, out_weight, preferred_element_type=jnp...  67 us
    all_gather x1, waiting for transfers between devices, body(): full_rows = lax.all_gather(hidden, 'wide', axis=1, tiled=True)  42.1 us
    all_gather x1, waiting for transfers between devices, body(): lax.all_gather(arrived, 'narrow', axis=0, tiled=True)  33.3 us
    all_to_all x1, blocking collectives, body(): lax.all_to_all(buffer.reshape(slot_count, capacity, feature_count), 'wide...  27.7 us
    all_to_all x1, waiting for transfers between devices, body(): lax.all_to_all(reduced, 'wide', split_axis=0, concat_axis=1, tiled=True)  23.9 us
    dot_general x1, matrix products, expert_terms(): jnp.einsum('gscf,sfd->gscd', active, w_down, preferred_element_type=jnp.f...  16.2 us
  transfers between devices with their start and end apart: 5, of which 5 were waited for; matrix products, arithmetic and copies ran while one was open for 1% of the time, Pallas kernels for 0%

commit v1 on v0

--- a/solution.py
+++ b/solution.py
@@ -6,6 +6,17 @@
 SPLIT = 2
 CAPD = 4
 epsilon = 1e-05
+
+
+def cut_along(x, dim, size):
+    before, after = (x.shape[:dim], x.shape[dim + 1 :])
+    return jnp.moveaxis(x.reshape(*before, size, -1, *after), dim, 0)
+
+
+def in_order(pieces, dim):
+    pieces = jnp.moveaxis(pieces, 0, dim)
+    shape = pieces.shape
+    return pieces.reshape(*shape[:dim], shape[dim] * shape[dim + 1], *shape[dim + 2 :])
 
 
 def layer_normed(values, gain):
@@ -163,13 +174,15 @@
         buffer.reshape(experts, 1, capacity, feature_count),
         (experts, SPLIT, capacity, feature_count),
     )
-    arrived = lax.all_to_all(
-        buffer.reshape(slot_count, capacity, feature_count),
-        "wide",
-        split_axis=0,
-        concat_axis=0,
-        tiled=True,
-    )
+    value = buffer.reshape(slot_count, capacity, feature_count)
+    devices, mine = (lax.axis_size("wide"), lax.axis_index("wide"))
+    parts = cut_along(value, 0, devices)
+    done = [parts[mine]]
+    for step in range(1, devices):
+        sent = parts[mine ^ step]
+        done.append(lax.ppermute(sent, "wide", [(i, i ^ step) for i in range(devices)]))
+    parts = jnp.stack(done)[mine ^ jnp.arange(devices)]
+    arrived = in_order(parts, 0)
     arrived = arrived.reshape(wide_count, slots_here, capacity, feature_count)
     partial_out = expert_terms(
         lax.all_gather(arrived, "narrow", axis=0, tiled=True), gate_weight, up_weight, down_weight

time: 456 us -> 458 us (level)
  blocking collectives: 121 us -> 93.4 us
  waiting for transfers between devices: 239 us -> 254 us
  starting transfers between devices: 5.82 us -> 17.3 us
    all_to_all x1 -> x0, blocking collectives: 27.7 us -> none  [body(): lax.all_to_all(buffer.reshape(slot_count, capacity, feature_count), 'wide...]
    ppermute x0 -> x7, waiting for transfers between devices: none -> 12.2 us  [body(): lax.ppermute(sent, 'wide', [(i, i ^ step) for i in range(devices)])]
    ppermute x0 -> x7, starting transfers between devices: none -> 11.4 us  [body(): lax.ppermute(sent, 'wide', [(i, i ^ step) for i in range(devices)])]
  transfers between devices with their start and end apart: 5 -> 12, of which waited for: 5 -> 8; matrix products, arithmetic and copies ran while one was open for 1% -> 1% of each run, Pallas kernels for 0% -> 0%
where the time goes in v1:
time: 458 us; the launch traced here: 457 us
  waiting for transfers between devices  254 us (55%)
  blocking collectives  93.4 us (20%)
  matrix products  54.8 us (12%)
  starting transfers between devices  17.3 us (4%)
  local copies, waits for them, and re-layouts  15.3 us (3%)
  between operations  13.6 us (3%)
  other arithmetic  9.13 us (2%)
    psum x1, blocking collectives, body(): key_cols, value_cols = lax.psum((key_term, value_term), 'wide')  71.9 us
    reduce_scatter x1, waiting for transfers between devices, body(): lax.psum_scatter(partial_out, 'narrow', scatter_dimension=0, tiled=True)  71.5 us
    reduce_scatter x1, waiting for transfers between devices, body(): lax.psum_scatter(jnp.dot(attended, out_weight, preferred_element_type=jnp...  67 us
    all_gather x1, waiting for transfers between devices, body(): full_rows = lax.all_gather(hidden, 'wide', axis=1, tiled=True)  42.1 us
    all_gather x1, waiting for transfers between devices, body(): lax.all_gather(arrived, 'narrow', axis=0, tiled=True)  36.3 us
    all_to_all x1, waiting for transfers between devices, body(): lax.all_to_all(reduced, 'wide', split_axis=0, concat_axis=1, tiled=True)  23.9 us
    dot_general x1, matrix products, expert_terms(): jnp.einsum('gscf,sfd->gscd', active, w_down, preferred_element_type=jnp.f...  16.2 us
    dot_general x1, matrix products, expert_terms(): jnp.einsum('gscd,sdf->gscf', arrived, w_gate, preferred_element_type=jnp....  16.1 us
  transfers between devices with their start and end apart: 12, of which 8 were waited for; matrix products, arithmetic and copies ran while one was open for 1% of the time, Pallas kernels for 0%

profile of v1, /device:TPU:0, one launch (start us, length us, event | category | flops | bytes accessed | tf_op | source)
XLA Modules:
  0.0 457.1 jit_solution(263289804408212877)
XLA Ops:
  8.3 0.9 constant_dynamic-slice_fusion.2
  9.4 42.1 %all-gather.4.cloned.1.call-done = bf16[128,4096]{1,0:T(8,128)(2,1)} async-done(((bf16[128,512]{1,0:T(8,128)(2,1)}), bf16[128,4096]{1,0:T(8,128)(2,1)}) %all-gather.4.cloned.1.call-update) | async-done | bytes 1048592 | tf_op jit(solution)/shard_map/all_gather | solution.py:114
  51.5 1.5 convert_reduce_fusion
  53.1 1.7 fusion.11
  55.2 3.0 fusion.21
  59.7 71.9 %all-reduce.2 = (bf16[128,1024]{1,0:T(8,128)(2,1)S(1)}, bf16[128,1024]{1,0:T(8,128)(2,1)S(1)}) all-reduce(f32[128,1024]{1,0:T(8,128)S(1)} %fusion.35, f32[128,1024]{1,0:T(8,128)S(1)} %fusion.37), channel_id=1, replica_groups=mesh['wide'=8,'narrow'=4] {'wide'}, use_global_device_ids=true, to_apply=%region_3.4 | all-reduce | flops 262144 | bytes 1572864 | tf_op jit(solution)/shard_map/psum | solution.py:127
  131.6 5.4 %all_gather.14 = bf16[512,128]{1,0:T(8,128)(2,1)S(1)} all-gather(bf16[128,128]{1,0:T(8,128)(2,1)S(1)} %dynamic-slice_convert_fusion), channel_id=1, replica_groups=mesh['wide'=8,'narrow'=4] {'narrow'}, dimensions={0}, use_global_device_ids=true | all-gather | bytes 163840 | tf_op jit(solution)/shard_map/all_gather | solution.py:135
  137.0 5.4 %all_gather.13 = bf16[512,128]{1,0:T(8,128)(2,1)S(1)} all-gather(bf16[128,128]{1,0:T(8,128)(2,1)S(1)} %dynamic-slice_convert_fusion.1), channel_id=1, replica_groups=mesh['wide'=8,'narrow'=4] {'narrow'}, dimensions={0}, use_global_device_ids=true | all-gather | bytes 163840 | tf_op jit(solution)/shard_map/all_gather | solution.py:136
  143.8 1.6 copy-done.3
  145.4 2.1 fusion.55
  149.0 67.0 %reduce-scatter.3.cloned.1.call-done = f32[16,4096]{1,0:T(8,128)} async-done(((f32[128,4096]{1,0:T(8,128)}), f32[16,4096]{1,0:T(8,128)}) %reduce-scatter.3.cloned.1.call-update) | async-done | bytes 262160 | tf_op jit(solution)/shard_map/reduce_scatter | solution.py:160
  216.0 1.1 convert_reduce_fusion.2
  219.5 2.0 collective-permute-start.1
  221.4 1.1 collective-permute-start.2
  222.5 1.3 collective-permute-start.3
  223.8 1.6 collective-permute-start.4
  225.4 2.1 collective-permute-start.5
  227.6 2.8 collective-permute-start.6
  230.9 8.9 %collective-permute-done.3 = bf16[4,4,4096]{2,1,0:T(4,128)(2,1)S(1)} collective-permute-done((bf16[4,4,4096]{2,1,0:T(4,128)(2,1)S(1)}, bf16[4,4,4096]{2,1,0:T(4,128)(2,1)S(1)}, u32[]{:S(2)}, u32[]{:S(2)}) %collective-permute-start.3) | collective-permute-done | bytes 131104 | tf_op jit(solution)/shard_map/ppermute | solution.py:183
  239.9 2.8 collective-permute-done.4
  243.0 1.4 gather_fusion
  244.4 1.6 copy.64
  246.2 36.3 %all-gather.6.cloned.1.call-done = bf16[32,4,4,4096]{3,0,2,1:T(8,128)(2,1)} async-done(((bf16[8,4,4,4096]{3,0,2,1:T(8,128)(2,1)}), bf16[32,4,4,4096]{3,0,2,1:T(8,128)(2,1)}) %all-gather.6.cloned.1.call-update) | async-done | bytes 4194320 | tf_op jit(solution)/shard_map/all_gather | solution.py:188
  282.5 16.1 %fusion.4 = f32[4,32,4,800]{3,1,2,0:T(8,128)} fusion(bf16[32,4,4,4096]{3,0,2,1:T(8,128)(2,1)} %all-gather.6.cloned.1.call-done, bf16[4,4096,800]{1,2,0:T(8,128)(2,1)} %param.25), kind=kOutput, calls=%fused_computation.7 | convolution fusion | flops 3355443200 | bytes 32047104 | tf_op jit(solution)/shard_map/gscd,sdf->gscf/dot_general | solution.py:67
  298.6 15.3 %fusion.15 = bf16[32,4,4,800]{3,0,2,1:T(8,128)(2,1)S(1)} fusion(f32[4,32,4,800]{3,1,2,0:T(8,128)} %fusion.4, bf16[32,4,4,4096]{3,0,2,1:T(8,128)(2,1)} %all-gather.6.cloned.1.call-done, bf16[4,4096,800]{1,2,0:T(8,128)(2,1)} %param.26), kind=kOutput, calls=%fused_computation.24 | convolution fusion | flops 3357900800 | bytes 32866304 | tf_op jit(solution)/shard_map/gscd,sdf->gscf/dot_general | solution.py:68
  313.9 16.2 %fusion.6 = f32[32,4,4,4096]{3,0,2,1:T(8,128)} fusion(bf16[32,4,4,800]{3,0,2,1:T(8,128)(2,1)S(1)} %fusion.15, bf16[4,800,4096]{2,1,0:T(8,128)(2,1)} %param.27), kind=kOutput, calls=%fused_computation.9 | convolution fusion | flops 3355443200 | bytes 35422208 | tf_op jit(solution)/shard_map/gscf,sfd->gscd/dot_general | solution.py:70
  330.1 71.5 %reduce-scatter.5.cloned.1.call-done = f32[8,4,4,4096]{3,0,2,1:T(8,128)} async-done(((f32[32,4,4,4096]{3,0,2,1:T(8,128)}), f32[8,4,4,4096]{3,0,2,1:T(8,128)}) %reduce-scatter.5.cloned.1.call-update) | async-done | bytes 2097168 | tf_op jit(solution)/shard_map/reduce_scatter | solution.py:190
  401.7 1.7 convert_element_type.112
  403.4 1.8 copy.65
  405.2 5.5 %all-to-all-start = ((bf16[8,4,4,4096]{3,2,1,0:T(4,128)(2,1)}), bf16[8,4,4,4096]{3,2,1,0:T(4,128)(2,1)S(1)}, u32[]{:S(2)}, u32[]{:S(2)}) async-start(bf16[8,4,4,4096]{3,2,1,0:T(4,128)(2,1)} %copy.65), calls=%async_computation.2 | async-start | bytes 2097152 | tf_op jit(solution)/shard_map/all_to_all | solution.py:193
  412.5 23.9 %all-to-all-done = bf16[8,4,4,4096]{3,2,1,0:T(4,128)(2,1)S(1)} async-done(((bf16[8,4,4,4096]{3,2,1,0:T(4,128)(2,1)}), bf16[8,4,4,4096]{3,2,1,0:T(4,128)(2,1)S(1)}, u32[]{:S(2)}, u32[]{:S(2)}) %all-to-all-start) | async-done | bytes 1048608 | tf_op jit(solution)/shard_map/all_to_all | solution.py:193
  439.3 10.7 %all_to_all.28 = bf16[16,8,512]{2,0,1:T(8,128)(2,1)S(1)} all-to-all(bf16[16,8,512]{2,0,1:T(8,128)(2,1)S(1)} %bitcast.137), channel_id=1, replica_groups=mesh['wide'=8,'narrow'=4] {'wide'}, dimensions={1} | all-to-all | bytes 262144 | tf_op jit(solution)/shard_map/all_to_all | solution.py:201
  (95 shorter events, 15.2 us)
Async XLA Ops:
  6.5 51.6 %copy-start = (bf16[512,1024]{1,0:T(8,128)(2,1)S(1)}, bf16[512,1024]{1,0:T(8,128)(2,1)}, u32[]{:S(2)}) copy-start(bf16[512,1024]{1,0:T(8,128)(2,1)} %param.17) | copy-start | bytes 3145732
  6.5 48.2 %copy-start.5 = (f32[4096]{0:T(1024)S(1)}, f32[4096]{0:T(1024)}, u32[]{:S(2)}) copy-start(f32[4096]{0:T(1024)} %param.15) | copy-start | bytes 49156
  6.5 45.0 %all-gather.4.cloned.1.call-start = ((), (), s32[]{:S(2)}) async-start(), calls=%async_computation.4 | async-start | bytes 1179648 | tf_op jit(solution)/shard_map/all_gather | solution.py:114
  7.3 208.7 %reduce-scatter.3.cloned.1.call-start = ((), (), s32[]{:S(2)}) async-start(), calls=%async_computation.5 | async-start | bytes 2359296 | tf_op jit(solution)/shard_map/reduce_scatter | solution.py:160
  51.5 3.2 copy-start.2
  58.1 1.2 copy-start.4
  143.2 2.2 copy-start.3
  147.5 0.7 copy-start.7
  147.5 69.8 %copy-start.6 = (f32[4096]{0:T(1024)S(1)}, f32[4096]{0:T(1024)}, u32[]{:S(2)}) copy-start(f32[4096]{0:T(1024)} %param.22) | copy-start | bytes 49156
  147.5 135.0 %all-gather.6.cloned.1.call-start = ((), (), s32[]{:S(2)}) async-start(), calls=%async_computation.7 | async-start | bytes 5242880 | tf_op jit(solution)/shard_map/all_gather | solution.py:188
  218.9 6.5 %collective-permute-start = (bf16[4,4,4096]{2,1,0:T(4,128)(2,1)S(1)}, bf16[4,4,4096]{2,1,0:T(4,128)(2,1)S(1)}, u32[]{:S(2)}, u32[]{:S(2)}) collective-permute-start(bf16[4,4,4096]{2,1,0:T(4,128)(2,1)S(1)} %get-tuple-element.21), channel_id=1, source_target_pairs={{0,4},{4,0},{8,12},{12,8},{16,20},{20,16},{24,28},{28,24},{1,5},{5... | collective-permute-start | bytes 393224 | tf_op jit(solution)/shard_map/ppermute | solution.py:183
  219.5 8.1 %collective-permute-start.1 = (bf16[4,4,4096]{2,1,0:T(4,128)(2,1)S(1)}, bf16[4,4,4096]{2,1,0:T(4,128)(2,1)S(1)}, u32[]{:S(2)}, u32[]{:S(2)}) collective-permute-start(bf16[4,4,4096]{2,1,0:T(4,128)(2,1)S(1)} %get-tuple-element.20), channel_id=1, source_target_pairs={{0,8},{4,12},{8,0},{12,4},{16,24},{20,28},{24,16},{28,20},{1,9},{5... | collective-permute-start | bytes 393224 | tf_op jit(solution)/shard_map/ppermute | solution.py:183
  221.4 9.4 %collective-permute-start.2 = (bf16[4,4,4096]{2,1,0:T(4,128)(2,1)S(1)}, bf16[4,4,4096]{2,1,0:T(4,128)(2,1)S(1)}, u32[]{:S(2)}, u32[]{:S(2)}) collective-permute-start(bf16[4,4,4096]{2,1,0:T(4,128)(2,1)S(1)} %get-tuple-element.19), channel_id=1, source_target_pairs={{0,12},{4,8},{8,4},{12,0},{16,28},{20,24},{24,20},{28,16},{1,13},{... | collective-permute-start | bytes 393224 | tf_op jit(solution)/shard_map/ppermute | solution.py:183
  222.5 17.4 %collective-permute-start.3 = (bf16[4,4,4096]{2,1,0:T(4,128)(2,1)S(1)}, bf16[4,4,4096]{2,1,0:T(4,128)(2,1)S(1)}, u32[]{:S(2)}, u32[]{:S(2)}) collective-permute-start(bf16[4,4,4096]{2,1,0:T(4,128)(2,1)S(1)} %get-tuple-element.18), channel_id=1, source_target_pairs={{0,16},{4,20},{8,24},{12,28},{16,0},{20,4},{24,8},{28,12},{1,17},{... | collective-permute-start | bytes 393224 | tf_op jit(solution)/shard_map/ppermute | solution.py:183
  223.8 19.0 %collective-permute-start.4 = (bf16[4,4,4096]{2,1,0:T(4,128)(2,1)S(1)}, bf16[4,4,4096]{2,1,0:T(4,128)(2,1)S(1)}, u32[]{:S(2)}, u32[]{:S(2)}) collective-permute-start(bf16[4,4,4096]{2,1,0:T(4,128)(2,1)S(1)} %get-tuple-element.17), channel_id=1, source_target_pairs={{0,20},{4,16},{8,28},{12,24},{16,4},{20,0},{24,12},{28,8},{1,21},{... | collective-permute-start | bytes 393224 | tf_op jit(solution)/shard_map/ppermute | solution.py:183
  225.4 17.4 %collective-permute-start.5 = (bf16[4,4,4096]{2,1,0:T(4,128)(2,1)S(1)}, bf16[4,4,4096]{2,1,0:T(4,128)(2,1)S(1)}, u32[]{:S(2)}, u32[]{:S(2)}) collective-permute-start(bf16[4,4,4096]{2,1,0:T(4,128)(2,1)S(1)} %get-tuple-element.16), channel_id=1, source_target_pairs={{0,24},{4,28},{8,16},{12,20},{16,8},{20,12},{24,0},{28,4},{1,25},{... | collective-permute-start | bytes 393224 | tf_op jit(solution)/shard_map/ppermute | solution.py:183
  227.6 15.3 %collective-permute-start.6 = (bf16[4,4,4096]{2,1,0:T(4,128)(2,1)S(1)}, bf16[4,4,4096]{2,1,0:T(4,128)(2,1)S(1)}, u32[]{:S(2)}, u32[]{:S(2)}) collective-permute-start(bf16[4,4,4096]{2,1,0:T(4,128)(2,1)S(1)} %get-tuple-element.15), channel_id=1, source_target_pairs={{0,28},{4,24},{8,20},{12,16},{16,12},{20,8},{24,4},{28,0},{1,29},{... | collective-permute-start | bytes 393224 | tf_op jit(solution)/shard_map/ppermute | solution.py:183
  246.0 155.7 %reduce-scatter.5.cloned.1.call-start = ((), (), s32[]{:S(2)}) async-start(), calls=%async_computation.6 | async-start | bytes 10485760 | tf_op jit(solution)/shard_map/reduce_scatter | solution.py:190
  403.4 7.8 %copy-start.8 = (bf16[4096,16]{0,1:T(8,128)(2,1)S(1)}, bf16[4096,16]{0,1:T(8,128)(2,1)}, u32[]{:S(2)}) copy-start(bf16[4096,16]{0,1:T(8,128)(2,1)} %param.23) | copy-start | bytes 393220
  405.2 31.2 %all-to-all-start = ((bf16[8,4,4,4096]{3,2,1,0:T(4,128)(2,1)}), bf16[8,4,4,4096]{3,2,1,0:T(4,128)(2,1)S(1)}, u32[]{:S(2)}, u32[]{:S(2)}) async-start(bf16[8,4,4,4096]{3,2,1,0:T(4,128)(2,1)} %copy.65), calls=%async_computation.2 | async-start | bytes 2097152 | tf_op jit(solution)/shard_map/all_to_all | solution.py:193
  437.4 13.2 %copy-start.1 = (bf16[512,1024]{1,0:T(8,128)(2,1)S(1)}, bf16[512,1024]{1,0:T(8,128)(2,1)}, u32[]{:S(2)}) copy-start(bf16[512,1024]{1,0:T(8,128)(2,1)} %param.17) | copy-start | bytes 3145732
Sparse Core Ops, SparseCore 0:
  9.4 42.1 all-gather.3
  147.6 68.2 reduce-scatter.2
  246.1 36.3 all-gather.5
  330.2 71.3 reduce-scatter.4
